TPU v7x, 256 devices: a whole 4x4x8 slice. The times are simulated.
256 devices in a mesh: ma: 64 (over y, z, core), vert: 4 (over x).
Axes of the slice: x: 4, y: 4, z: 8, core: 2. Of those that a mesh axis runs over, the one named last changes fastest.
Arguments:
- trial_block: bfloat16 [128, 512, 4, 1024], P('vert', 'ma'), may hold values from -6 to 6
- legendre: bfloat16 [512, 2, 256, 1024], P('ma'), may hold values from -0.1875 to 0.1875
- order_slot: int32 [512], replicated, may hold values from 0 to 511, each once
- cycle_start: int32 [256], replicated, may hold values from 0 to 1023
- cycle_count: int32 [256], replicated, may hold values from 0 to 1024, as said below
- cycle_weight: float32 [256], replicated, may hold values from 4 to 32
Outputs:
- new_basis: bfloat16 [128, 512, 4, 1024], P('vert', 'ma')
- ritz_matrix: float32 [128, 128], replicated
Inputs may be any that keep to these rules, and one draw needn't show every extreme that they name: `cycle_count`: exactly 64 consecutive cycles have a nonzero count, and one of them has 1024.
All inputs are finite; a program needn't handle non-finite values.
Results may differ from a plain program's by a relative error of at most 0.0073.
The roundings to bfloat16 on the way count: a program that leaves them out, or rounds other values in their place, can miss the bound.
Values may be sent and summed in bfloat16 or wider, within the bound.
No kernel may reach another device: no remote copies, remote signals or barrier semaphores. Data moves between devices by JAX's collectives and lax.ppermute only.
A program may use at most 192 MiB of HBM per device.

v0:
```python
import functools
import math

import jax
import jax.numpy as jnp
from jax import lax
from jax.sharding import Mesh
from jax.sharding import PartitionSpec as P

MA = ("ma_0", "ma_1", "ma_2")


def by_axis(value, axes):
    return functools.reduce(lax.psum, axes, value)


def combine_fields(products):
    first_kind = products[:, 0]
    second_kind = products[:, 1]
    return jnp.stack(
        [
            first_kind[..., 0] + second_kind[..., 3],
            first_kind[..., 1] - second_kind[..., 2],
            second_kind[..., 1] - first_kind[..., 2],
            -second_kind[..., 0] - first_kind[..., 3],
        ],
        axis=-1,
    )


def adjoint_terms(returned):
    gtc = returned[..., 0]
    gts = returned[..., 1]
    gpc = returned[..., 2]
    gps = returned[..., 3]
    first_kind = jnp.stack([gtc, gts, -gpc, -gps], axis=-1)
    second_kind = jnp.stack([-gps, gpc, -gts, gtc], axis=-1)
    return jnp.stack([first_kind, second_kind], axis=1)


def fourier_tables(order_slot, longitudes, orders_total):
    longitude = jnp.arange(longitudes, dtype=jnp.int32)
    phases = longitude[:, None] * order_slot[None, :] % longitudes
    angles = phases.astype(jnp.float32) * (2.0 * math.pi / longitudes)
    scale = 1.0 / math.sqrt(orders_total)
    return (
        (jnp.cos(angles) * scale).astype(jnp.bfloat16),
        (jnp.sin(angles) * scale).astype(jnp.bfloat16),
    )


def synthesize(trial_block, table_rows):
    orders_here = trial_block.shape[1]
    vectors = trial_block.shape[0]
    products = lax.dot_general(
        table_rows, trial_block, (((3,), (3,)), ((0,), (1,))), preferred_element_type=jnp.float32
    )
    fields = combine_fields(products).astype(jnp.bfloat16)
    return fields.reshape(orders_here, table_rows.shape[2], vectors * 4)


def cycle_transform(cycle_fields, cycle_first, order_slot, cycle_start, cycle_count, cycle_weight):
    orders_total, cycles_here, columns = cycle_fields.shape
    vectors = columns // 4
    longitudes = 2 * orders_total
    pieces = cycle_fields.reshape(orders_total, cycles_here, vectors, 4)
    cosine, sines = fourier_tables(order_slot, longitudes, orders_total)
    grid_values = jnp.einsum(
        "jo,orkc->rckj", cosine, pieces[..., 0::2], preferred_element_type=jnp.float32
    )
    grid_values = grid_values + jnp.einsum(
        "jo,orkc->rckj", sines, pieces[..., 1::2], preferred_element_type=jnp.float32
    )
    starts = lax.dynamic_slice_in_dim(cycle_start, cycle_first, cycles_here)
    counts = lax.dynamic_slice_in_dim(cycle_count, cycle_first, cycles_here)
    weights = lax.dynamic_slice_in_dim(cycle_weight, cycle_first, cycles_here)
    longitude = jnp.arange(longitudes, dtype=jnp.int32)
    inside = ((longitude[None, :] - starts[:, None]) % longitudes < counts[:, None]).astype(
        jnp.float32
    )
    factor = inside * weights[:, None]
    weighted = (grid_values * factor[:, None, None, :]).astype(jnp.bfloat16)
    back_cos = jnp.einsum("jo,rckj->orkc", cosine, weighted, preferred_element_type=jnp.float32)
    back_sin = jnp.einsum("jo,rckj->orkc", sines, weighted, preferred_element_type=jnp.float32)
    returned = jnp.stack(
        [back_cos[..., 0], back_sin[..., 0], back_cos[..., 1], back_sin[..., 1]], axis=-1
    )
    return returned.astype(jnp.bfloat16).reshape(orders_total, cycles_here, columns)


def analyse(order_fields, table_rows, vectors):
    orders_here, cycles_here, columns = order_fields.shape
    pieces = order_fields.reshape(orders_here, cycles_here, vectors, 4)
    adjoint = adjoint_terms(pieces).reshape(orders_here, 2, cycles_here, columns)
    applied = lax.dot_general(
        adjoint, table_rows, (((1, 2), (1, 2)), ((0,), (0,))), preferred_element_type=jnp.float32
    )
    applied = applied.reshape(orders_here, vectors, 4, table_rows.shape[3])
    return applied.transpose(1, 0, 2, 3).astype(jnp.bfloat16)


def gram_terms(trial_part, applied_part):
    trial_flat = trial_part.reshape(trial_part.shape[0], -1)
    applied_flat = applied_part.reshape(applied_part.shape[0], -1)
    dims = (((1,), (1,)), ((), ()))
    gram_trial = lax.dot_general(trial_flat, trial_flat, dims, preferred_element_type=jnp.float32)
    cross = lax.dot_general(trial_flat, applied_flat, dims, preferred_element_type=jnp.float32)
    gram_applied = lax.dot_general(
        applied_flat, applied_flat, dims, preferred_element_type=jnp.float32
    )
    return (gram_trial, cross, gram_applied)


def finish_ritz(totals, coefficients):
    gram_trial = totals[0] / coefficients
    cross = totals[1] / coefficients
    gram_applied = totals[2] / coefficients
    factor_trial = jnp.linalg.cholesky(gram_trial)
    half_solved = lax.linalg.triangular_solve(factor_trial, cross, left_side=True, lower=True)
    ritz_matrix = lax.linalg.triangular_solve(
        factor_trial, half_solved.T, left_side=True, lower=True
    ).T
    factor_applied = jnp.linalg.cholesky(gram_applied)
    identity = jnp.eye(gram_applied.shape[0], dtype=jnp.float32)
    mixing = lax.linalg.triangular_solve(factor_applied, identity, left_side=True, lower=True)
    return (ritz_matrix, mixing.astype(jnp.bfloat16))


def shards(trial_block, legendre, order_slot, cycle_start, cycle_count, cycle_weight):
    vectors = trial_block.shape[0]
    orders_here = trial_block.shape[1]
    degrees = trial_block.shape[3]
    cycles_total = legendre.shape[2]
    live_cycles = cycles_total // 4
    started = jnp.cumsum((cycle_count > 0).astype(jnp.int32))
    first_cycle = jnp.sum((started == 0).astype(jnp.int32))
    table_rows = lax.dynamic_slice_in_dim(legendre, first_cycle, live_cycles, 2)
    fields = synthesize(trial_block, table_rows)
    cycle_fields = lax.all_to_all(fields, MA, split_axis=1, concat_axis=0, tiled=True)
    per_device = cycle_fields.shape[1]
    cycle_first = first_cycle + lax.axis_index(MA) * per_device
    returned = cycle_transform(
        cycle_fields, cycle_first, order_slot, cycle_start, cycle_count, cycle_weight
    )
    order_fields = lax.all_to_all(returned, MA, split_axis=0, concat_axis=1, tiled=True)
    applied = analyse(order_fields, table_rows, vectors)
    coefficients = lax.axis_size(MA) * orders_here * 4 * degrees
    trial_all, applied_all = (
        lax.all_gather(trial_block, "vert", axis=0, tiled=True),
        lax.all_gather(applied, "vert", axis=0, tiled=True),
    )
    totals = jax.tree.map(lambda part: by_axis(part, MA), gram_terms(trial_all, applied_all))
    ritz_matrix, mixing = finish_ritz(totals, coefficients)
    mix_rows = lax.dynamic_slice_in_dim(mixing, lax.axis_index("vert") * vectors, vectors, 0)
    mixed = jnp.dot(
        mix_rows, applied_all.reshape(applied_all.shape[0], -1), preferred_element_type=jnp.float32
    )
    new_basis = mixed.reshape(trial_block.shape).astype(jnp.bfloat16)
    return (new_basis, ritz_matrix)


def solution(mesh):
    split = Mesh(
        mesh.devices.reshape(4, 8, 2, mesh.shape["vert"]), ("ma_0", "ma_1", "ma_2", "vert")
    )
    placed = (P("vert", MA, None, None), P(MA, None, None, None), P(), P(), P(), P())
    return jax.shard_map(
        shards,
        mesh=split,
        in_specs=placed,
        out_specs=(P("vert", MA, None, None), P()),
        check_vma=False,
    )
```

profile of v0, /device:TPU:1, one launch (start us, length us, event | category | flops | bytes accessed | tf_op | source)
XLA Modules:
  0.0 424.8 jit_solution(12173860981991819685)
XLA Ops:
  7.2 4.1 copy.54
  15.2 3.4 fusion.5
  19.0 0.9 copy.41
  19.9 13.1 %all-to-all-start = ((bf16[8,64,128]{2,0,1:T(8,128)(2,1)}), bf16[8,64,128]{2,0,1:T(8,128)(2,1)S(1)}, u32[]{:S(2)}, u32[]{:S(2)}) async-start(bf16[8,64,128]{2,0,1:T(8,128)(2,1)} %copy.41), calls=%async_computation | async-start | bytes 262144 | tf_op jit(solution)/shard_map/all_to_all | solution.py:139
  36.1 1.9 fusion.54
  38.0 5.4 %all-to-all-done = bf16[8,64,128]{2,0,1:T(8,128)(2,1)S(1)} async-done(((bf16[8,64,128]{2,0,1:T(8,128)(2,1)}), bf16[8,64,128]{2,0,1:T(8,128)(2,1)S(1)}, u32[]{:S(2)}, u32[]{:S(2)}) %all-to-all-start) | async-done | bytes 131104 | tf_op jit(solution)/shard_map/all_to_all | solution.py:139
  43.4 2.9 copy.42
  46.4 2.4 reshape.136
  49.9 7.8 %fusion.27 = f32[32,2,1024]{2,0,1:T(8,128)S(1)} fusion(s32[512]{0:T(512)S(1)} %copy-done.3, bf16[512,1,32,2]{0,3,2,1:T(2,128)(2,1)S(1)} %slice.92), kind=kOutput, calls=%fused_computation.37 | convolution fusion | flops 75497472 | bytes 329728 | tf_op jit(solution)/shard_map/jo,orkc->rckj/dot_general | solution.py:68
  57.7 8.2 %fusion.19 = bf16[2,32,1024]{2,1,0:T(8,128)(2,1)S(1)} fusion(f32[32,2,1024]{2,0,1:T(8,128)S(1)} %fusion.27, s32[512]{0:T(512)S(1)} %copy-done.3, f32[1024]{0:T(1024)S(1)} %fusion.54, bf16[512,1,32,2]{0,3,2,1:T(2,128)(2,1)S(1)} %slice.93), kind=kOutput, calls=%fused_computation.25 | convolution fusion | flops 75694080 | bytes 464896 | tf_op jit(solution)/shard_map/jo,orkc->rckj/dot_general | solution.py:71
  66.0 8.4 %fusion.20 = bf16[512,1,32,2]{0,2,3,1:T(8,128)(2,1)S(1)} fusion(bf16[2,32,1024]{2,1,0:T(8,128)(2,1)S(1)} %fusion.19, s32[512]{0:T(512)S(1)} %copy-done.3), kind=kOutput, calls=%fused_computation.28 | convolution fusion | flops 75530240 | bytes 198656 | tf_op jit(solution)/shard_map/jo,rckj->orkc/dot_general | solution.py:83
  74.4 8.5 %fusion.21 = bf16[512,1,32,2]{0,2,3,1:T(8,128)(2,1)S(1)} fusion(bf16[2,32,1024]{2,1,0:T(8,128)(2,1)S(1)} %fusion.19, s32[512]{0:T(512)S(1)} %copy-done.3), kind=kOutput, calls=%fused_computation.29 | convolution fusion | flops 75530240 | bytes 198656 | tf_op jit(solution)/shard_map/jo,rckj->orkc/dot_general | solution.py:84
  84.5 15.3 %all_to_all.30 = bf16[64,2,512]{2,1,0:T(2,128)(2,1)S(1)} all-to-all(bf16[64,2,512]{2,1,0:T(2,128)(2,1)S(1)} %reshape.165), channel_id=1, replica_groups=mesh['ma_0'=4,'ma_1'=8,'ma_2'=2,'vert'=4] {'ma_0','ma_1','ma_2'}, dimensions={0} | all-to-all | bytes 262144 | tf_op jit(solution)/shard_map/all_to_all | solution.py:145
  100.8 2.4 bitcast_convert_fusion
  103.2 2.2 convert_element_type.66
  105.4 3.6 copy.82
  109.1 8.7 %convolution_bitcast_fusion.3 = f32[128,128]{0,1:T(8,128)} fusion(bf16[128,8,4,1024]{3,0,2,1:T(8,128)(2,1)} %all-gather.5.cloned.1.call-done), kind=kOutput, calls=%fused_computation.33 | convolution fusion | flops 1073741824 | bytes 8454144 | tf_op jit(solution)/shard_map/dot_general | solution.py:106
  117.8 72.5 %all-gather.3.cloned.1.call-done = bf16[128,8,4,1024]{3,0,2,1:T(8,128)(2,1)} async-done(((bf16[32,8,4,1024]{3,0,2,1:T(8,128)(2,1)}), bf16[128,8,4,1024]{3,0,2,1:T(8,128)(2,1)}) %all-gather.3.cloned.1.call-update) | async-done | bytes 8388624 | tf_op jit(solution)/shard_map/all_gather | solution.py:150
  190.3 8.9 %convolution_bitcast_fusion.2 = f32[128,128]{0,1:T(8,128)} fusion(bf16[128,8,4,1024]{3,0,2,1:T(8,128)(2,1)} %all-gather.3.cloned.1.call-done, bf16[128,8,4,1024]{3,0,2,1:T(8,128)(2,1)} %all-gather.5.cloned.1.call-done), kind=kOutput, calls=%fused_computation.32 | convolution fusion | flops 1073741824 | bytes 16842752 | tf_op jit(solution)/shard_map/dot_general | solution.py:107
  199.2 3.0 convolution_bitcast_fusion.4
  202.2 45.8 %all-reduce.9.cloned.1.call-done = (f32[128,128]{0,1:T(8,128)}, f32[128,128]{0,1:T(8,128)}, f32[128,128]{0,1:T(8,128)}) async-done(((f32[128,128]{0,1:T(8,128)}, f32[128,128]{0,1:T(8,128)}, f32[128,128]{0,1:T(8,128)}), (f32[128,128]{0,1:T(8,128)}, f32[128,128]{0,1:T(8,128)}, f32[128,128]{0,1:T(8,128)})) %all-reduce.9.cloned.1.call-update) | async-done | bytes 196624 | tf_op jit(solution)/shard_map/psum | solution.py:14
  248.1 72.5 %all-reduce.7.cloned.1.call-done = (f32[128,128]{0,1:T(8,128)}, f32[128,128]{0,1:T(8,128)}, f32[128,128]{0,1:T(8,128)}) async-done(((f32[128,128]{0,1:T(8,128)}, f32[128,128]{0,1:T(8,128)}, f32[128,128]{0,1:T(8,128)}), (f32[128,128]{0,1:T(8,128)}, f32[128,128]{0,1:T(8,128)}, f32[128,128]{0,1:T(8,128)})) %all-reduce.7.cloned.1.call-update) | async-done | bytes 196624 | tf_op jit(solution)/shard_map/psum | solution.py:14
  320.6 11.6 %copy.53 = bf16[128,8,4,1024]{0,3,2,1:T(8,128)(2,1)} copy(bf16[128,8,4,1024]{3,0,2,1:T(8,128)(2,1)} %all-gather.3.cloned.1.call-done) | data formatting | bytes 16777216 | tf_op jit(solution)/shard_map/all_gather | solution.py:150
  332.2 24.3 %all-reduce.11.cloned.1.call-done = (f32[128,128]{0,1:T(8,128)}, f32[128,128]{0,1:T(8,128)}, f32[128,128]{0,1:T(8,128)}) async-done(((f32[128,128]{0,1:T(8,128)}, f32[128,128]{0,1:T(8,128)}, f32[128,128]{0,1:T(8,128)}), (f32[128,128]{0,1:T(8,128)}, f32[128,128]{0,1:T(8,128)}, f32[128,128]{0,1:T(8,128)})) %all-reduce.11.cloned.1.call-update) | async-done | bytes 196624 | tf_op jit(solution)/shard_map/psum | solution.py:14
  357.4 0.9 fusion.40
  358.3 11.7 %cholesky.55 = f32[128,128]{1,0:T(8,128)S(1)} custom-call(f32[128,128]{1,0:T(8,128)S(1)} %fusion.40), custom_call_target="Cholesky" | custom-call | tf_op jit(solution)/shard_map/jit(cholesky)/cholesky | solution.py:118
  371.3 9.8 %custom-call.9 = f32[1,128,128]{1,2,0:T(8,128)S(1)} custom-call(f32[1,128,128]{2,1,0:T(8,128)S(1)} %fusion.37), custom_call_target="InvertDiagBlocksLowerTriangular" | custom-call | tf_op jit(solution)/shard_map/triangular_solve/custom-call.0 | solution.py:120
  381.1 1.1 convolution_bitcast_fusion.1
  385.1 11.7 %cholesky.44 = f32[128,128]{1,0:T(8,128)S(1)} custom-call(f32[128,128]{1,0:T(8,128)S(1)} %fusion.43), custom_call_target="Cholesky" | custom-call | tf_op jit(solution)/shard_map/jit(cholesky)/cholesky | solution.py:123
  398.1 10.1 %custom-call.7 = f32[1,128,128]{1,2,0:T(8,128)S(1)} custom-call(f32[1,128,128]{2,1,0:T(8,128)S(1)} %fusion.36), custom_call_target="InvertDiagBlocksLowerTriangular" | custom-call | tf_op jit(solution)/shard_map/triangular_solve/custom-call.0 | solution.py:125
  408.5 6.4 %fusion.11 = bf16[32,8,4,1024]{3,0,2,1:T(8,128)(2,1)S(1)} fusion(bf16[128,8,4,1024]{0,3,2,1:T(8,128)(2,1)} %copy.53, bf16[128,128]{1,0:T(8,128)(2,1)S(1)} %fusion.41, s32[]{:T(128)S(6)} %select_n.37), kind=kOutput, calls=%fused_computation.18 | convolution fusion | flops 269484032 | bytes 10493956 | tf_op jit(solution)/shard_map/dot_general | solution.py:155
  414.9 2.9 copy.57
  (68 shorter events, 15.2 us)
Async XLA Ops:
  7.2 101.9 %all-gather.5.cloned.1.call-start = ((), (), s32[]{:S(2)}) async-start(), calls=%async_computation.3 | async-start | bytes 10485760 | tf_op jit(solution)/shard_map/all_gather | solution.py:149
  11.3 0.7 copy-start.2
  11.3 3.9 copy-start.1
  18.6 16.4 %copy-start.4 = (s32[256]{0:T(256)S(1)}, s32[256]{0:T(256)}, u32[]{:S(2)}) copy-start(s32[256]{0:T(256)} %param.12) | copy-start | bytes 3076
  18.6 17.0 %copy-start.5 = (f32[256]{0:T(256)S(1)}, f32[256]{0:T(256)}, u32[]{:S(2)}) copy-start(f32[256]{0:T(256)} %param.14) | copy-start | bytes 3076
  19.9 23.5 %all-to-all-start = ((bf16[8,64,128]{2,0,1:T(8,128)(2,1)}), bf16[8,64,128]{2,0,1:T(8,128)(2,1)S(1)}, u32[]{:S(2)}, u32[]{:S(2)}) async-start(bf16[8,64,128]{2,0,1:T(8,128)(2,1)} %copy.41), calls=%async_computation | async-start | bytes 262144 | tf_op jit(solution)/shard_map/all_to_all | solution.py:139
  33.1 157.3 %all-gather.3.cloned.1.call-start = ((), (), s32[]{:S(2)}) async-start(), calls=%async_computation.2 | async-start | bytes 10485760 | tf_op jit(solution)/shard_map/all_gather | solution.py:150
  43.4 6.5 %copy-start.3 = (s32[512]{0:T(512)S(1)}, s32[512]{0:T(512)}, u32[]{:S(2)}) copy-start(s32[512]{0:T(512)} %param.11) | copy-start | bytes 6148
  109.0 139.0 %all-reduce.9.cloned.1.call-start = ((), (), s32[]{:S(2)}) async-start(), calls=%async_computation.5 | async-start | bytes 393216 | tf_op jit(solution)/shard_map/psum | solution.py:14
  190.3 8.9 %copy-start = (bf16[128,8,4,1024]{3,0,2,1:T(8,128)(2,1)S(1)}, bf16[128,8,4,1024]{3,0,2,1:T(8,128)(2,1)}, u32[]{:S(2)}) copy-start(bf16[128,8,4,1024]{3,0,2,1:T(8,128)(2,1)} %all-gather.3.cloned.1.call-done) | copy-start | bytes 25165828
  202.2 118.4 %all-reduce.7.cloned.1.call-start = ((), (), s32[]{:S(2)}) async-start(), calls=%async_computation.4 | async-start | bytes 393216 | tf_op jit(solution)/shard_map/psum | solution.py:14
  248.0 108.5 %all-reduce.11.cloned.1.call-start = ((), (), s32[]{:S(2)}) async-start(), calls=%async_computation.6 | async-start | bytes 393216 | tf_op jit(solution)/shard_map/psum | solution.py:14
Sparse Core Ops, SparseCore 0:
  11.5 89.4 all-gather.4
  109.1 81.1 all-gather.2
  202.3 45.6 all-reduce.8
  250.5 69.9 all-reduce.6
  323.2 33.2 all-reduce.10
where the time goes:
time: 430 us; the launch traced here: 425 us
  waiting for transfers between devices  221 us (51%)
  matrix products  67.4 us (16%)
  other arithmetic  53.3 us (12%)
  local copies, waits for them, and re-layouts  37.1 us (9%)
  between operations  17.2 us (4%)
  blocking collectives  15.3 us (4%)
  starting transfers between devices  13.9 us (3%)
    psum x3, waiting for transfers between devices, by_axis(): return functools.reduce(lax.psum, axes, value)  143 us
    all_gather x1, waiting for transfers between devices, shards(): lax.all_gather(applied, 'vert', axis=0, tiled=True)  72.5 us
    all_to_all x1, blocking collectives, shards(): lax.all_to_all(returned, MA, split_axis=0, concat_axis=1, tiled=True)  15.3 us
    all_to_all x1, starting transfers between devices, shards(): lax.all_to_all(fields, MA, split_axis=1, concat_axis=0, tiled=True)  13.1 us
    another operation x3, other arithmetic, finish_ritz(): factor_applied = jnp.linalg.cholesky(gram_applied)  12.4 us
    another operation x3, other arithmetic, finish_ritz(): factor_trial = jnp.linalg.cholesky(gram_trial)  12.4 us
    all_gather x1, local copies, waits for them, and re-layouts, shards(): lax.all_gather(applied, 'vert', axis=0, tiled=True)  11.6 us
    another operation x2, other arithmetic, finish_ritz(): lax.linalg.triangular_solve(factor_applied, identity, left_side=True, low...  10.7 us
  transfers between devices with their start and end apart: 6, of which 5 were waited for; matrix products, arithmetic and copies ran while one was open for 19% of the time, Pallas kernels for 0%

commit v1 on v0

v1 whole, which is shorter than its diff:
```python
import functools
import math

import jax
import jax.numpy as jnp
from jax import lax
from jax.experimental import pallas as pl
from jax.experimental.pallas import tpu as pltpu
from jax.sharding import Mesh
from jax.sharding import PartitionSpec as P

MA = ("ma_0", "ma_1", "ma_2")
ALL = MA + ("vert",)
F32 = jnp.float32
BF16 = jnp.bfloat16
WINDOW = 80
NT = (((1,), (1,)), ((), ()))
NN = (((1,), (0,)), ((), ()))


def ring(size, shift):
    return [(i, (i + shift) % size) for i in range(size)]


def dot(a, b, dims=NN):
    return lax.dot_general(a, b, dims, preferred_element_type=F32)


def dot_high(a, b, dims=NN):
    return lax.dot_general(
        a, b, dims, precision=lax.Precision.HIGHEST, preferred_element_type=F32
    )


def window_copy(legendre, leg_v, sem, s, start):
    return pltpu.make_async_copy(
        legendre.at[s, :, pl.ds(start, WINDOW), :], leg_v.at[s], sem.at[s]
    )


def synthesize_kernel(
    where, trial, legendre, fields, tt, tr_v, leg_v, tt_v, prod, sem_t, sem_l, sem_o
):
    orders = trial.shape[1]
    vectors = trial.shape[0]
    start = pl.multiple_of(where[0], 16)
    shift = where[1]
    for s in range(orders):
        pltpu.make_async_copy(trial.at[:, s], tr_v.at[s], sem_t.at[s]).start()
        window_copy(legendre, leg_v, sem_l, s, start).start()
    rows = 4 * vectors
    i = lax.broadcasted_iota(jnp.int32, (rows, rows), 0)
    j = lax.broadcasted_iota(jnp.int32, (rows, rows), 1)
    by_part = (j == (i % vectors) * 4 + i // vectors).astype(BF16)
    for s in range(orders):
        pltpu.make_async_copy(trial.at[:, s], tr_v.at[s], sem_t.at[s]).wait()
        x = tr_v[s].reshape(rows, tr_v.shape[3])
        t = dot(by_part, x).astype(BF16)
        t0, t1, t2, t3 = (t[c * vectors : (c + 1) * vectors] for c in range(4))
        for c, part in enumerate((t0, t1, t2, t3)):
            tt_v[s, c] = part
        pltpu.make_async_copy(tt_v.at[s], tt.at[s], sem_o.at[s]).start()
        first_kind = jnp.concatenate([t0, t1, -t3, -t2], axis=0)
        second_kind = jnp.concatenate([t3, -t2, -t0, t1], axis=0)
        window_copy(legendre, leg_v, sem_l, s, start).wait()
        prod[s * WINDOW : (s + 1) * WINDOW] = dot(leg_v[s, 0], first_kind, NT) + dot(
            leg_v[s, 1], second_kind, NT
        )
    for r in range(fields.shape[0]):
        fields[r] = prod[pl.ds(shift + r, orders, stride=WINDOW), :].astype(BF16)
    for s in range(orders):
        pltpu.make_async_copy(tt_v.at[s], tt.at[s], sem_o.at[s]).wait()


def synthesize(where, trial, legendre, cycles):
    vectors, orders, _, degrees = trial.shape
    return pl.pallas_call(
        synthesize_kernel,
        out_shape=(
            jax.ShapeDtypeStruct((cycles, orders, 4 * vectors), BF16),
            jax.ShapeDtypeStruct((orders, 4, vectors, degrees), BF16),
        ),
        in_specs=[
            pl.BlockSpec(memory_space=pltpu.SMEM),
            pl.BlockSpec(memory_space=pl.ANY),
            pl.BlockSpec(memory_space=pl.ANY),
        ],
        out_specs=(
            pl.BlockSpec(memory_space=pltpu.VMEM),
            pl.BlockSpec(memory_space=pl.ANY),
        ),
        scratch_shapes=[
            pltpu.VMEM((orders, vectors, 4, degrees), BF16),
            pltpu.VMEM((orders, 2, WINDOW, degrees), BF16),
            pltpu.VMEM((orders, 4, vectors, degrees), BF16),
            pltpu.VMEM((orders * WINDOW, 4 * vectors), F32),
            pltpu.SemaphoreType.DMA((orders,)),
            pltpu.SemaphoreType.DMA((orders,)),
            pltpu.SemaphoreType.DMA((orders,)),
        ],
        compiler_params=pltpu.CompilerParams(vmem_limit_bytes=40 << 20),
        cost_estimate=pl.CostEstimate(
            flops=600_000_000, bytes_accessed=8 << 20, transcendentals=0
        ),
        name="synthesize",
    )(where, trial, legendre)


def tables_kernel(slot, cosine, sines):
    orders, longitudes = cosine.shape
    lanes = 128
    scale = 1.0 / math.sqrt(orders)
    step = 2.0 * math.pi / longitudes
    m = slot[...]
    near = lax.broadcasted_iota(jnp.int32, (orders, lanes), 1)
    near = ((m * near) & (longitudes - 1)).astype(F32) * step
    near_cos = jnp.cos(near) * scale
    near_sin = jnp.sin(near) * scale
    blocks = longitudes // lanes
    eighth = lax.broadcasted_iota(jnp.int32, (orders, lanes), 1) & (blocks - 1)
    far = ((m * eighth * lanes) & (longitudes - 1)).astype(F32) * step
    far_cos = jnp.cos(far)
    far_sin = jnp.sin(far)
    for b in range(blocks):
        a = far_cos[:, b : b + 1]
        c = far_sin[:, b : b + 1]
        cosine[:, b * lanes : (b + 1) * lanes] = (a * near_cos - c * near_sin).astype(BF16)
        sines[:, b * lanes : (b + 1) * lanes] = (c * near_cos + a * near_sin).astype(BF16)


def fourier_tables(order_slot):
    orders = order_slot.shape[0]
    shape = jax.ShapeDtypeStruct((orders, 2 * orders), BF16)
    return pl.pallas_call(
        tables_kernel,
        out_shape=(shape, shape),
        compiler_params=pltpu.CompilerParams(vmem_limit_bytes=32 << 20),
        cost_estimate=pl.CostEstimate(
            flops=10_000_000, bytes_accessed=2 << 20, transcendentals=300_000
        ),
        name="tables",
    )(order_slot[:, None])


def transform_kernel(received, cosine, sines, factor, returned):
    columns = received.shape[1]
    part = columns // 4
    ft = received[...].astype(F32).T.astype(BF16)
    with_cos = jnp.concatenate([ft[:part], ft[3 * part :]], axis=0)
    with_sin = ft[part : 3 * part]
    grid = dot(with_cos, cosine[...]) + dot(with_sin, sines[...])
    weighted = (grid * factor[...]).astype(BF16)
    colat, azimuth = weighted[:part], weighted[part:]
    none = jnp.zeros_like(colat)
    back = dot(
        cosine[...], jnp.concatenate([colat, none, none, azimuth], axis=0), NT
    ) + dot(sines[...], jnp.concatenate([none, colat, azimuth, none], axis=0), NT)
    returned[...] = back.astype(BF16)


def cycle_transform(received, cosine, sines, factor):
    return pl.pallas_call(
        transform_kernel,
        out_shape=jax.ShapeDtypeStruct(received.shape, BF16),
        compiler_params=pltpu.CompilerParams(vmem_limit_bytes=40 << 20),
        cost_estimate=pl.CostEstimate(
            flops=600_000_000, bytes_accessed=3 << 20, transcendentals=0
        ),
        name="transform",
    )(received, cosine, sines, factor)


def analyse_kernel(
    where, got0, got1, got2, got3, legendre, tt, applied, gram,
    wide, adj, leg_v, tt_v, app_v, sem_l, sem_t, sem_o,
):
    orders, _, vectors, _ = tt.shape
    columns = 4 * vectors
    start = pl.multiple_of(where[0], 16)
    shift = where[1]
    for s in range(orders):
        window_copy(legendre, leg_v, sem_l, s, start).start()
        pltpu.make_async_copy(tt.at[s], tt_v.at[s], sem_t.at[s]).start()
    gots = (got0, got1, got2, got3)
    for e, got in enumerate(gots):
        wide[e] = got[...].astype(F32)
    adj[...] = jnp.zeros_like(adj)
    lane = lax.broadcasted_iota(jnp.int32, (1, columns), 1) // vectors
    one = jnp.ones((1, columns), F32)
    sign0 = jnp.where(lane < 2, one, -one)
    sign1 = jnp.where((lane == 0) | (lane == 3), -one, one)
    cycles = got0.shape[0] // orders
    block = {0: 0, 1: 1, 3: 2, 2: 3}
    total = jnp.zeros(gram.shape, F32)
    for s in range(orders):
        for e in range(4):
            x = wide[e, pl.ds(s, cycles, stride=orders), :]
            base = e * 2 * WINDOW + shift
            adj[pl.ds(base, cycles), :] = x * sign0
            adj[pl.ds(base + WINDOW, cycles), :] = pltpu.roll(x, columns // 2, 1) * sign1
        a = jnp.concatenate(
            [adj[e * 2 * WINDOW : (e + 1) * 2 * WINDOW].T for e in range(4)], axis=0
        ).astype(BF16)
        window_copy(legendre, leg_v, sem_l, s, start).wait()
        rows = dot(a, leg_v[s].reshape(2 * WINDOW, leg_v.shape[3])).astype(BF16)
        pltpu.make_async_copy(tt.at[s], tt_v.at[s], sem_t.at[s]).wait()
        for c in range(4):
            b = block[c] * vectors
            own = [rows[e * columns + b : e * columns + b + vectors] for e in range(4)]
            every = jnp.concatenate(own, axis=0)
            app_v[s, c] = every
            total = total + dot(jnp.concatenate([tt_v[s, c], own[0]], axis=0), every, NT)
        pltpu.make_async_copy(app_v.at[s], applied.at[s], sem_o.at[s]).start()
    gram[...] = total
    for s in range(orders):
        pltpu.make_async_copy(app_v.at[s], applied.at[s], sem_o.at[s]).wait()


def analyse(where, gots, legendre, tt):
    orders, _, vectors, degrees = tt.shape
    cycles_rows, columns = gots[0].shape
    vmem = pl.BlockSpec(memory_space=pltpu.VMEM)
    hbm = pl.BlockSpec(memory_space=pl.ANY)
    return pl.pallas_call(
        analyse_kernel,
        out_shape=(
            jax.ShapeDtypeStruct((orders, 4, 4 * vectors, degrees), BF16),
            jax.ShapeDtypeStruct((2 * vectors, 4 * vectors), F32),
        ),
        in_specs=[pl.BlockSpec(memory_space=pltpu.SMEM)] + [vmem] * 4 + [hbm] * 2,
        out_specs=(hbm, vmem),
        scratch_shapes=[
            pltpu.VMEM((4, cycles_rows, columns), F32),
            pltpu.VMEM((4 * 2 * WINDOW, columns), F32),
            pltpu.VMEM((orders, 2, WINDOW, degrees), BF16),
            pltpu.VMEM((orders, 4, vectors, degrees), BF16),
            pltpu.VMEM((orders, 4, 4 * vectors, degrees), BF16),
            pltpu.SemaphoreType.DMA((orders,)),
            pltpu.SemaphoreType.DMA((orders,)),
            pltpu.SemaphoreType.DMA((orders,)),
        ],
        compiler_params=pltpu.CompilerParams(vmem_limit_bytes=48 << 20),
        cost_estimate=pl.CostEstimate(
            flops=2_000_000_000, bytes_accessed=14 << 20, transcendentals=0
        ),
        name="analyse",
    )(where, *gots, legendre, tt)


def trial_gram(blocks):
    def body(b0, b1, b2, b3, out):
        total = jnp.zeros(out.shape, F32)
        for s in range(b0.shape[0]):
            for c in range(4):
                x = jnp.concatenate([b[s, c] for b in (b0, b1, b2, b3)], axis=0)
                total = total + dot(x, x, NT)
        out[...] = total

    rows = 4 * blocks[0].shape[2]
    return pl.pallas_call(
        body,
        out_shape=jax.ShapeDtypeStruct((rows, rows), F32),
        compiler_params=pltpu.CompilerParams(vmem_limit_bytes=32 << 20),
        cost_estimate=pl.CostEstimate(
            flops=300_000_000, bytes_accessed=2 << 20, transcendentals=0
        ),
        name="trial_gram",
    )(*blocks)


def inverse_factors_kernel(trial_gram_ref, cross, applied_gram_ref, ritz, mixing, work):
    n = cross.shape[0]
    row = lax.broadcasted_iota(jnp.int32, (n, 2 * n), 0)
    col = lax.broadcasted_iota(jnp.int32, (n, 2 * n), 1)
    identity = (col == row + n).astype(F32)
    for which, ref in enumerate((trial_gram_ref, applied_gram_ref)):
        work[which] = identity
        work[which, :, :n] = ref[...]
    column = lax.broadcasted_iota(jnp.int32, (1, 2 * n), 1)
    index = lax.broadcasted_iota(jnp.int32, (n, 1), 0)

    def step(j, _):
        for which in range(2):
            m = work[which]
            line = work[which, pl.ds(j, 1), :]
            pivot = jnp.sum(jnp.where(column == j, line, 0.0), axis=1, keepdims=True)
            scaled = line / pivot
            multiple = jnp.sum(jnp.where(col == j, m, 0.0), axis=1, keepdims=True)
            multiple = jnp.where(index > j, multiple, 0.0)
            work[which] = m - multiple * scaled
            work[which, pl.ds(j, 1), :] = line * lax.rsqrt(pivot)
        return 0

    lax.fori_loop(0, n, step, 0)
    inverse_trial = work[0, :, n:]
    half = dot_high(inverse_trial, cross[...])
    ritz[...] = dot_high(half, inverse_trial, NT)
    mixing[...] = work[1, :, n:].astype(BF16)


def finish_ritz(gram_trial, cross, gram_applied):
    n = cross.shape[0]
    return pl.pallas_call(
        inverse_factors_kernel,
        out_shape=(
            jax.ShapeDtypeStruct((n, n), F32),
            jax.ShapeDtypeStruct((n, n), BF16),
        ),
        scratch_shapes=[pltpu.VMEM((2, n, 2 * n), F32)],
        name="factors",
    )(gram_trial, cross, gram_applied)


def mix_kernel(weights, applied, out):
    vectors = out.shape[0]
    x = applied[0].reshape(applied.shape[1] * applied.shape[2], applied.shape[3])
    y = dot(weights[...], x).astype(BF16)
    out[:, 0] = y.reshape(vectors, 4, applied.shape[3])


def mix(weights, applied):
    orders, _, everyone, degrees = applied.shape
    vectors = everyone // 4
    return pl.pallas_call(
        mix_kernel,
        grid=(orders,),
        out_shape=jax.ShapeDtypeStruct((vectors, orders, 4, degrees), BF16),
        in_specs=[
            pl.BlockSpec(weights.shape, lambda s: (0, 0)),
            pl.BlockSpec((1, 4, everyone, degrees), lambda s: (s, 0, 0, 0)),
        ],
        out_specs=pl.BlockSpec((vectors, 1, 4, degrees), lambda s: (0, s, 0, 0)),
        compiler_params=pltpu.CompilerParams(vmem_limit_bytes=32 << 20),
        cost_estimate=pl.CostEstimate(
            flops=1_100_000_000, bytes_accessed=10 << 20, transcendentals=0
        ),
        name="mix",
    )(weights, applied)


def shards(trial_block, legendre, order_slot, cycle_start, cycle_count, cycle_weight):
    vectors, orders, _, degrees = trial_block.shape
    cycles_total = legendre.shape[2]
    live = cycles_total // 4
    groups = 4
    everyone = groups * vectors
    columns = 4 * vectors
    me = lax.axis_index("vert")
    home = lax.axis_index(MA)
    owners = live
    longitudes = 2 * order_slot.shape[0]

    cycle_index = jnp.arange(cycles_total, dtype=jnp.int32)
    first = jnp.min(jnp.where(cycle_count > 0, cycle_index, cycles_total - live))
    start = jnp.minimum(first // 16 * 16, cycles_total - WINDOW)
    where = jnp.stack([start, first - start])

    fields, tt = synthesize(where, trial_block, legendre, live)
    received = lax.all_to_all(fields, MA, split_axis=0, concat_axis=0, tiled=True)
    cosine, sines = fourier_tables(order_slot)

    pair = orders // groups

    def pair_of(d):
        return lax.dynamic_slice_in_dim(tt, (me + d) % groups * pair, pair, 0)

    blocks = [pair_of(0)] + [
        lax.ppermute(pair_of(d), "vert", ring(groups, d)) for d in range(1, groups)
    ]

    mine = cycle_index == first + home
    count, begin = (
        jnp.sum(jnp.where(mine, x, 0)) for x in (cycle_count, cycle_start)
    )
    weight = jnp.sum(jnp.where(mine, cycle_weight, 0.0))
    longitude = jnp.arange(longitudes, dtype=jnp.int32)
    inside = (longitude - begin) % longitudes < count
    factor = jnp.where(inside, weight, 0.0)[None, :]
    returned = cycle_transform(
        received.reshape(owners * orders, columns), cosine, sines, factor
    )
    order_fields = lax.all_to_all(
        returned.reshape(owners, orders, columns), MA, split_axis=0, concat_axis=0, tiled=True
    )
    order_fields = order_fields.reshape(owners * orders, columns)
    gots = [order_fields] + [
        lax.ppermute(order_fields, "vert", ring(groups, -d)) for d in range(1, groups)
    ]

    share = trial_gram(blocks)
    rows_home = []
    for d in range(groups):
        rows = share[d * vectors : (d + 1) * vectors]
        rows = jnp.concatenate(
            [
                rows[:, (d - e) % groups * vectors : ((d - e) % groups + 1) * vectors]
                for e in range(groups)
            ],
            axis=1,
        )
        rows_home.append(rows if d == 0 else lax.ppermute(rows, "vert", ring(groups, -d)))
    trial_rows = sum(rows_home[1:], rows_home[0])

    applied, gram = analyse(where, gots, legendre, tt)
    half = everyone // 2
    packed = jnp.concatenate(
        [gram, jnp.concatenate([trial_rows[:, :half], trial_rows[:, half:]], axis=0)], axis=1
    )
    chunks = lax.all_to_all(packed, MA, split_axis=0, concat_axis=0, tiled=True)
    summed = jnp.sum(chunks, axis=0, keepdims=True)
    everywhere = owners * groups
    summed = lax.all_to_all(
        jnp.broadcast_to(summed, (everywhere, packed.shape[1])),
        ALL,
        split_axis=0,
        concat_axis=0,
        tiled=True,
    )
    summed = summed.reshape(owners, groups, packed.shape[1]) / (owners * orders * 4 * degrees)
    crosses, applieds, trials = [], [], []
    for v in range(groups):
        s = summed[:, v]
        t = jnp.concatenate([s[:vectors, everyone:], s[vectors:, everyone:]], axis=1)
        for into, rows in (
            (crosses, s[:vectors, :everyone]),
            (applieds, s[vectors:, :everyone]),
            (trials, t),
        ):
            into.append(jnp.roll(rows, v * vectors, axis=1))
    ritz_matrix, mixing = finish_ritz(
        *(jnp.concatenate(x, axis=0) for x in (trials, crosses, applieds))
    )
    mine_rows = lax.dynamic_slice_in_dim(mixing, me * vectors, vectors, 0)
    twice = jnp.concatenate([mine_rows, mine_rows], axis=1)
    mine_rows = lax.dynamic_slice_in_dim(twice, me * vectors, everyone, 1)
    spread = jnp.where(
        jnp.arange(4)[None, :, None, None] == jnp.arange(4)[None, None, :, None],
        mine_rows[:, None, None, :],
        jnp.zeros((), BF16),
    ).reshape(4 * vectors, 4 * everyone)
    new_basis = mix(spread, applied)
    return (new_basis, ritz_matrix)


def solution(mesh):
    split = Mesh(
        mesh.devices.reshape(4, 8, 2, mesh.shape["vert"]), ("ma_0", "ma_1", "ma_2", "vert")
    )
    placed = (P("vert", MA, None, None), P(MA, None, None, None), P(), P(), P(), P())
    return jax.shard_map(
        shards,
        mesh=split,
        in_specs=placed,
        out_specs=(P("vert", MA, None, None), P()),
        check_vma=False,
    )
```

time: 430 us -> 175 us (0.41); the launches traced: 425 us -> 175 us
  waiting for transfers between devices: 221 us -> 26.9 us
  matrix products: 67.4 us -> 0 us
  Pallas kernels: 0 us -> 62.2 us
  other arithmetic: 53.3 us -> 7.92 us
  starting transfers between devices: 13.9 us -> 39.6 us
  local copies, waits for them, and re-layouts: 37.1 us -> 16.5 us
  between operations: 17.2 us -> 4.93 us
    psum x3 -> x0, waiting for transfers between devices: 143 us -> none  [by_axis(): return functools.reduce(lax.psum, axes, value)]
    all_gather x2 -> x0, waiting for transfers between devices: 72.5 us -> none  [the longest x1 72.5 us: shards(): lax.all_gather(applied, 'vert', axis=0, tiled=True)]
    dot_general x10 -> x0, matrix products: 65.7 us -> none  [the longest x1 8.86 us: gram_terms(): lax.dot_general(trial_flat, applied_flat, dims, preferred_element_type=jn...]
    pallas_call x0 -> x7, Pallas kernels: none -> 62.2 us  [the longest x1 29.6 us: finish_ritz(): pl.pallas_call(inverse_factors_kernel, out_shape=(jax.ShapeDtypeStruct((n...]
    another operation x17 -> x1, other arithmetic: 46.6 us -> 0.08 us  [shards(): where = jnp.stack([start, first - start])]
    all_to_all x1 -> x3, waiting for transfers between devices: 5.39 us -> 21.7 us  [the longest x1 15.7 us: shards(): lax.all_to_all(jnp.broadcast_to(summed, (everywhere, packed.shape[1])), A...]
    all_to_all x1 -> x3, starting transfers between devices: 13.1 us -> 27.9 us  [the longest x1 13.2 us: shards(): lax.all_to_all(fields, MA, split_axis=0, concat_axis=0, tiled=True)]
    ppermute x0 -> x9, starting transfers between devices: none -> 11.7 us  [the longest x3 4.43 us: shards(): lax.ppermute(pair_of(d), 'vert', ring(groups, d))]
  transfers between devices with their start and end apart: 6 -> 12, of which waited for: 5 -> 5; matrix products, arithmetic and copies ran while one was open for 19% -> 2% of each run, Pallas kernels for 0% -> 4%
where the time goes in v1:
time: 175 us
  Pallas kernels  62.2 us (36%)
  starting transfers between devices  39.6 us (23%)
  waiting for transfers between devices  26.9 us (15%)
  blocking collectives  16.7 us (10%)
  local copies, waits for them, and re-layouts  16.5 us (9%)
  other arithmetic  7.92 us (5%)
  between operations  4.93 us (3%)
    pallas_call x1, Pallas kernels, finish_ritz(): pl.pallas_call(inverse_factors_kernel, out_shape=(jax.ShapeDtypeStruct((n...  29.6 us
    all_to_all x1, blocking collectives, shards(): chunks = lax.all_to_all(packed, MA, split_axis=0, concat_axis=0, tiled=True)  16.7 us
    all_to_all x1, waiting for transfers between devices, shards(): lax.all_to_all(jnp.broadcast_to(summed, (everywhere, packed.shape[1])), A...  15.7 us
    pallas_call x1, Pallas kernels, analyse(): pl.pallas_call(analyse_kernel, out_shape=(jax.ShapeDtypeStruct((orders, 4...  13.4 us
    all_to_all x1, starting transfers between devices, shards(): lax.all_to_all(fields, MA, split_axis=0, concat_axis=0, tiled=True)  13.2 us
    unnamed x27, local copies, waits for them, and re-layouts  12.8 us
    all_to_all x1, starting transfers between devices, shards(): lax.all_to_all(returned.reshape(owners, orders, columns), MA, split_axis=...  9.01 us
    pallas_call x1, Pallas kernels, synthesize(): pl.pallas_call(synthesize_kernel, out_shape=(jax.ShapeDtypeStruct((cycles...  7.76 us
  transfers between devices with their start and end apart: 12, of which 5 were waited for; matrix products, arithmetic and copies ran while one was open for 2% of the time, Pallas kernels for 4%

profile of v1, /device:TPU:1, one launch (start us, length us, event | category | flops | bytes accessed | tf_op | source)
XLA Modules:
  0.0 174.8 jit_solution(1349373722071820709)
XLA Ops:
  0.7 1.3 fusion.9
  5.4 3.4 %copy-done = bf16[8,2,256,1024]{3,2,1,0:T(8,128)(2,1)S(1)} copy-done((bf16[8,2,256,1024]{3,2,1,0:T(8,128)(2,1)S(1)}, bf16[8,2,256,1024]{3,2,1,0:T(8,128)(2,1)}, u32[]{:S(2)}) %copy-start) | copy-done | bytes 8388632
  8.7 1.6 copy-done.2
  10.3 7.8 %synthesize.1 = (bf16[64,8,128]{2,1,0:T(8,128)(2,1)}, bf16[8,4,32,1024]{3,2,1,0:T(8,128)(2,1)S(1)}) custom-call(s32[2]{0:T(128)S(1)} %pad_add_fusion.where, bf16[32,8,4,1024]{3,2,1,0:T(4,128)(2,1)S(1)} %copy-done.2, bf16[8,2,256,1024]{3,2,1,0:T(8,128)(2,1)S(1)} %copy-done), custom_call_target="tpu_custom_call" | custom-call | flops 600000000 | bytes 8388608 | tf_op jit(solution)/shard_map/synthesize/pallas_call | solution.py:77
  18.1 1.2 constant_dynamic-slice_fusion.1
  19.4 3.3 %collective-permute-start.5 = (bf16[2,4,32,1024]{3,2,1,0:T(8,128)(2,1)}, bf16[2,4,32,1024]{3,2,1,0:T(8,128)(2,1)S(1)}, u32[]{:S(2)}, u32[]{:S(2)}) collective-permute-start(bf16[2,4,32,1024]{3,2,1,0:T(8,128)(2,1)} %get-tuple-element.18), channel_id=1, source_target_pairs={{0,3},{1,0},{2,1},{3,2},{4,7},{5,4},{6,5},{7,6},{8,11},{9,8},{10,9... | collective-permute-start | bytes 1572872 | tf_op jit(solution)/shard_map/ppermute | solution.py:368
  23.8 13.2 %all-to-all-start = ((bf16[64,8,128]{2,1,0:T(8,128)(2,1)}), bf16[64,8,128]{2,1,0:T(8,128)(2,1)S(1)}, u32[]{:S(2)}, u32[]{:S(2)}) async-start(bf16[64,8,128]{2,1,0:T(8,128)(2,1)} %get-tuple-element.10), calls=%async_computation | async-start | bytes 262144 | tf_op jit(solution)/shard_map/all_to_all | solution.py:359
  38.4 3.2 %tables.1 = (bf16[512,1024]{1,0:T(8,128)(2,1)S(1)}, bf16[512,1024]{1,0:T(8,128)(2,1)S(1)}) custom-call(s32[512,1]{1,0:T(8,128)S(1)} %copy.13.slot), custom_call_target="tpu_custom_call" | custom-call | flops 10000000 | bytes 2097152 | tf_op jit(solution)/shard_map/tables/pallas_call | solution.py:134
  41.6 1.0 copy-done.3
  42.6 1.0 copy-done.5
  44.2 1.8 %compare_select_fusion.2.factor = f32[1,1024]{1,0:T(1,128)S(1)} fusion(f32[]{:T(128)} %select_reduce_fusion, s32[]{:T(128)} %get-tuple-element.68, s32[]{:T(128)} %get-tuple-element.69), kind=kLoop, calls=%fused_computation.27 | loop fusion | flops 14336 | bytes 4108 | tf_op jit(solution)/shard_map/jit(_where)/select_n | solution.py:378
  46.0 1.3 all-to-all-done
  47.4 1.2 copy-done.4
  48.6 1.2 copy-done.6
  49.8 1.9 %transform.1 = bf16[512,128]{1,0:T(8,128)(2,1)} custom-call(bf16[512,128]{1,0:T(8,128)(2,1)S(1)} %bitcast.29, bf16[512,1024]{1,0:T(8,128)(2,1)S(1)} %copy-done.4, bf16[512,1024]{1,0:T(8,128)(2,1)S(1)} %copy-done.6, f32[1,1024]{1,0:T(1,128)S(1)} %compare_select_fusion.2.factor), custom_call_target="tpu_custom_call" | custom-call | flops 600000000 | bytes 3145728 | tf_op jit(solution)/shard_map/transform/pallas_call | solution.py:162
  51.7 9.0 %all-to-all-start.1 = ((bf16[64,8,128]{2,1,0:T(8,128)(2,1)}), bf16[64,8,128]{2,1,0:T(8,128)(2,1)S(1)}, u32[]{:S(2)}, u32[]{:S(2)}) async-start(bf16[64,8,128]{2,1,0:T(8,128)(2,1)} %bitcast.4), calls=%async_computation.1 | async-start | bytes 262144 | tf_op jit(solution)/shard_map/all_to_all | solution.py:382
  60.7 1.9 %trial_gram.1 = f32[128,128]{1,0:T(8,128)S(1)} custom-call(bf16[2,4,32,1024]{3,2,1,0:T(8,128)(2,1)S(1)} %get-tuple-element.21.b0, bf16[2,4,32,1024]{3,2,1,0:T(8,128)(2,1)} %collective-permute-done.3.b1, bf16[2,4,32,1024]{3,2,1,0:T(8,128)(2,1)} %collective-permute-done.4.b2, bf16[2,4,32,1024]{3,2,1,0:T(8,128)(2,1)S(1)} %collective-permute-done.5.b3), custom_call_target="tpu_custom_call" | custom-call | flops 300000000 | bytes 2097152 | tf_op jit(solution)/shard_map/trial_gram/pallas_call | solution.py:260
  62.8 2.1 %collective-permute-start.6 = (f32[32,128]{1,0:T(8,128)S(1)}, f32[32,128]{1,0:T(8,128)S(1)}, u32[]{:S(2)}, u32[]{:S(2)}) collective-permute-start(f32[32,128]{1,0:T(8,128)S(1)} %pad_maximum_fusion.2), channel_id=1, source_target_pairs={{0,3},{1,0},{2,1},{3,2},{4,7},{5,4},{6,5},{7,6},{8,11},{9,8},{10,9... | collective-permute-start | bytes 49160 | tf_op jit(solution)/shard_map/ppermute | solution.py:401
  65.0 1.3 collective-permute-start.7
  66.4 4.7 %all-to-all-done.1 = bf16[64,8,128]{2,1,0:T(8,128)(2,1)S(1)} async-done(((bf16[64,8,128]{2,1,0:T(8,128)(2,1)}), bf16[64,8,128]{2,1,0:T(8,128)(2,1)S(1)}, u32[]{:S(2)}, u32[]{:S(2)}) %all-to-all-start.1) | async-done | bytes 131104 | tf_op jit(solution)/shard_map/all_to_all | solution.py:382
  71.0 1.5 collective-permute-start.2
  72.6 1.7 collective-permute-start.1
  75.1 1.8 %collective-permute-done.2.got3 = bf16[512,128]{1,0:T(8,128)(2,1)S(1)} collective-permute-done((bf16[512,128]{1,0:T(8,128)(2,1)S(1)}, bf16[512,128]{1,0:T(8,128)(2,1)S(1)}, u32[]{:S(2)}, u32[]{:S(2)}) %collective-permute-start.2) | collective-permute-done | bytes 131104 | tf_op jit(solution)/shard_map/ppermute | solution.py:387
  76.9 3.4 %collective-permute-done.1.got2 = bf16[512,128]{1,0:T(8,128)(2,1)S(1)} collective-permute-done((bf16[512,128]{1,0:T(8,128)(2,1)S(1)}, bf16[512,128]{1,0:T(8,128)(2,1)S(1)}, u32[]{:S(2)}, u32[]{:S(2)}) %collective-permute-start.1) | collective-permute-done | bytes 131104 | tf_op jit(solution)/shard_map/ppermute | solution.py:387
  80.3 13.4 %analyse.1 = (bf16[8,4,128,1024]{3,2,1,0:T(8,128)(2,1)}, f32[64,128]{1,0:T(8,128)S(1)}) custom-call(s32[2]{0:T(128)S(1)} %pad_add_fusion.where, bf16[512,128]{1,0:T(8,128)(2,1)S(1)} %bitcast.28, bf16[512,128]{1,0:T(8,128)(2,1)S(1)} %collective-permute-done.got1, bf16[512,128]{1,0:T(8,128)(2,1)S(1)} %collective-permute-done.1.got2, ...), custom_call_target="tpu_custom_call" | custom-call | flops 2000000000 | bytes 14680064 | tf_op jit(solution)/shard_map/analyse/pallas_call | solution.py:224
  93.9 16.7 %all_to_all.25 = f32[64,1,192]{2,1,0:T(1,128)S(1)} all-to-all(f32[64,1,192]{2,1,0:T(1,128)S(1)} %copy.14), channel_id=1, replica_groups=mesh['ma_0'=4,'ma_1'=8,'ma_2'=2,'vert'=4] {'ma_0','ma_1','ma_2'}, dimensions={0} | all-to-all | bytes 98304 | tf_op jit(solution)/shard_map/all_to_all | solution.py:409
  110.7 0.8 broadcast_in_dim.57
  111.5 5.7 %all-to-all-start.3 = ((f32[256,1,192]{2,1,0:T(1,128)}), f32[256,1,192]{2,1,0:T(1,128)S(1)}, u32[]{:S(2)}, u32[]{:S(2)}) async-start(f32[256,1,192]{2,1,0:T(1,128)} %broadcast_in_dim.57), calls=%async_computation.3 | async-start | bytes 524288 | tf_op jit(solution)/shard_map/all_to_all | solution.py:412
  117.2 15.7 %all-to-all-done.3 = f32[256,1,192]{2,1,0:T(1,128)S(1)} async-done(((f32[256,1,192]{2,1,0:T(1,128)}), f32[256,1,192]{2,1,0:T(1,128)S(1)}, u32[]{:S(2)}, u32[]{:S(2)}) %all-to-all-start.3) | async-done | bytes 196640 | tf_op jit(solution)/shard_map/all_to_all | solution.py:412
  136.4 29.6 %factors.1 = (f32[128,128]{1,0:T(8,128)}, bf16[128,128]{1,0:T(8,128)(2,1)}) custom-call(f32[128,128]{1,0:T(8,128)} %fusion.1.trial_gram_ref, f32[128,128]{1,0:T(8,128)} %maximum_maximum_fusion.cross, f32[128,128]{1,0:T(8,128)} %maximum_maximum_fusion.1.applied_gram_ref), custom_call_target="tpu_custom_call" | custom-call | tf_op jit(solution)/shard_map/factors/pallas_call | solution.py:303
  167.0 3.4 %copy-done.1 = bf16[8,4,128,1024]{3,2,1,0:T(8,128)(2,1)S(1)} copy-done((bf16[8,4,128,1024]{3,2,1,0:T(8,128)(2,1)S(1)}, bf16[8,4,128,1024]{3,2,1,0:T(8,128)(2,1)}, u32[]{:S(2)}) %copy-start.1) | copy-done | bytes 8388632
  170.4 4.4 %mix.1 = bf16[32,8,4,1024]{3,2,1,0:T(4,128)(2,1)} custom-call(bf16[128,512]{1,0:T(8,128)(2,1)S(1)} %bitcast.30, bf16[8,4,128,1024]{3,2,1,0:T(8,128)(2,1)S(1)} %copy-done.1), custom_call_target="tpu_custom_call" | custom-call | flops 1100000000 | bytes 10485760 | tf_op jit(solution)/shard_map/mix/pallas_call | solution.py:324
  (63 shorter events, 8.3 us)
Async XLA Ops:
  5.4 3.4 %copy-start = (bf16[8,2,256,1024]{3,2,1,0:T(8,128)(2,1)S(1)}, bf16[8,2,256,1024]{3,2,1,0:T(8,128)(2,1)}, u32[]{:S(2)}) copy-start(bf16[8,2,256,1024]{3,2,1,0:T(8,128)(2,1)} %legendre.3) | copy-start | bytes 25165828
  8.7 1.6 copy-start.2
  18.1 19.6 %copy-start.10 = (f32[256]{0:T(256)S(1)}, f32[256]{0:T(256)}, u32[]{:S(2)}) copy-start(f32[256]{0:T(256)} %param.11) | copy-start | bytes 3076
  18.1 20.2 %copy-start.7 = (s32[512]{0:T(512)S(1)}, s32[512]{0:T(512)}, u32[]{:S(2)}) copy-start(s32[512]{0:T(512)} %param.8) | copy-start | bytes 6148
  18.1 25.5 %copy-start.8 = (s32[256]{0:T(256)S(1)}, s32[256]{0:T(256)}, u32[]{:S(2)}) copy-start(s32[256]{0:T(256)} %param.10) | copy-start | bytes 3076
  18.1 25.5 %copy-start.9 = (s32[256]{0:T(256)S(1)}, s32[256]{0:T(256)}, u32[]{:S(2)}) copy-start(s32[256]{0:T(256)} %param.9) | copy-start | bytes 3076
  19.4 41.3 %collective-permute-start.5 = (bf16[2,4,32,1024]{3,2,1,0:T(8,128)(2,1)}, bf16[2,4,32,1024]{3,2,1,0:T(8,128)(2,1)S(1)}, u32[]{:S(2)}, u32[]{:S(2)}) collective-permute-start(bf16[2,4,32,1024]{3,2,1,0:T(8,128)(2,1)} %get-tuple-element.18), channel_id=1, source_target_pairs={{0,3},{1,0},{2,1},{3,2},{4,7},{5,4},{6,5},{7,6},{8,11},{9,8},{10,9... | collective-permute-start | bytes 1572872 | tf_op jit(solution)/shard_map/ppermute | solution.py:368
  22.7 38.0 %collective-permute-start.4 = (bf16[2,4,32,1024]{3,2,1,0:T(8,128)(2,1)}, bf16[2,4,32,1024]{3,2,1,0:T(8,128)(2,1)}, u32[]{:S(2)}, u32[]{:S(2)}) collective-permute-start(bf16[2,4,32,1024]{3,2,1,0:T(8,128)(2,1)} %get-tuple-element.19), channel_id=1, source_target_pairs={{0,2},{1,3},{2,0},{3,1},{4,6},{5,7},{6,4},{7,5},{8,10},{9,11},{10,... | collective-permute-start | bytes 1572872 | tf_op jit(solution)/shard_map/ppermute | solution.py:368
  23.2 37.5 %collective-permute-start.3 = (bf16[2,4,32,1024]{3,2,1,0:T(8,128)(2,1)}, bf16[2,4,32,1024]{3,2,1,0:T(8,128)(2,1)}, u32[]{:S(2)}, u32[]{:S(2)}) collective-permute-start(bf16[2,4,32,1024]{3,2,1,0:T(8,128)(2,1)} %get-tuple-element.20), channel_id=1, source_target_pairs={{0,1},{1,2},{2,3},{3,0},{4,5},{5,6},{6,7},{7,4},{8,9},{9,10},{10,1... | collective-permute-start | bytes 1572872 | tf_op jit(solution)/shard_map/ppermute | solution.py:368
  23.8 23.5 %all-to-all-start = ((bf16[64,8,128]{2,1,0:T(8,128)(2,1)}), bf16[64,8,128]{2,1,0:T(8,128)(2,1)S(1)}, u32[]{:S(2)}, u32[]{:S(2)}) async-start(bf16[64,8,128]{2,1,0:T(8,128)(2,1)} %get-tuple-element.10), calls=%async_computation | async-start | bytes 262144 | tf_op jit(solution)/shard_map/all_to_all | solution.py:359
  41.6 1.0 copy-start.3
  42.6 1.0 copy-start.5
  47.4 1.2 copy-start.4
  48.6 1.2 copy-start.6
  51.7 19.4 %all-to-all-start.1 = ((bf16[64,8,128]{2,1,0:T(8,128)(2,1)}), bf16[64,8,128]{2,1,0:T(8,128)(2,1)S(1)}, u32[]{:S(2)}, u32[]{:S(2)}) async-start(bf16[64,8,128]{2,1,0:T(8,128)(2,1)} %bitcast.4), calls=%async_computation.1 | async-start | bytes 262144 | tf_op jit(solution)/shard_map/all_to_all | solution.py:382
  62.8 11.5 %collective-permute-start.6 = (f32[32,128]{1,0:T(8,128)S(1)}, f32[32,128]{1,0:T(8,128)S(1)}, u32[]{:S(2)}, u32[]{:S(2)}) collective-permute-start(f32[32,128]{1,0:T(8,128)S(1)} %pad_maximum_fusion.2), channel_id=1, source_target_pairs={{0,3},{1,0},{2,1},{3,2},{4,7},{5,4},{6,5},{7,6},{8,11},{9,8},{10,9... | collective-permute-start | bytes 49160 | tf_op jit(solution)/shard_map/ppermute | solution.py:401
  65.0 10.0 %collective-permute-start.7 = (f32[32,128]{1,0:T(8,128)S(1)}, f32[32,128]{1,0:T(8,128)S(1)}, u32[]{:S(2)}, u32[]{:S(2)}) collective-permute-start(f32[32,128]{1,0:T(8,128)S(1)} %pad_maximum_fusion.3), channel_id=1, source_target_pairs={{0,2},{1,3},{2,0},{3,1},{4,6},{5,7},{6,4},{7,5},{8,10},{9,11},{10,... | collective-permute-start | bytes 49160 | tf_op jit(solution)/shard_map/ppermute | solution.py:401
  66.3 8.6 %collective-permute-start.8 = (f32[32,128]{1,0:T(8,128)S(1)}, f32[32,128]{1,0:T(8,128)S(1)}, u32[]{:S(2)}, u32[]{:S(2)}) collective-permute-start(f32[32,128]{1,0:T(8,128)S(1)} %pad_maximum_fusion.4), channel_id=1, source_target_pairs={{0,1},{1,2},{2,3},{3,0},{4,5},{5,6},{6,7},{7,4},{8,9},{9,10},{10,1... | collective-permute-start | bytes 49160 | tf_op jit(solution)/shard_map/ppermute | solution.py:401
  71.0 5.9 %collective-permute-start.2 = (bf16[512,128]{1,0:T(8,128)(2,1)S(1)}, bf16[512,128]{1,0:T(8,128)(2,1)S(1)}, u32[]{:S(2)}, u32[]{:S(2)}) collective-permute-start(bf16[512,128]{1,0:T(8,128)(2,1)S(1)} %bitcast.25), channel_id=1, source_target_pairs={{0,1},{1,2},{2,3},{3,0},{4,5},{5,6},{6,7},{7,4},{8,9},{9,10},{10,1... | collective-permute-start | bytes 393224 | tf_op jit(solution)/shard_map/ppermute | solution.py:387
  72.6 7.8 %collective-permute-start.1 = (bf16[512,128]{1,0:T(8,128)(2,1)S(1)}, bf16[512,128]{1,0:T(8,128)(2,1)S(1)}, u32[]{:S(2)}, u32[]{:S(2)}) collective-permute-start(bf16[512,128]{1,0:T(8,128)(2,1)S(1)} %bitcast.26), channel_id=1, source_target_pairs={{0,2},{1,3},{2,0},{3,1},{4,6},{5,7},{6,4},{7,5},{8,10},{9,11},{10,... | collective-permute-start | bytes 393224 | tf_op jit(solution)/shard_map/ppermute | solution.py:387
  74.3 6.0 %collective-permute-start = (bf16[512,128]{1,0:T(8,128)(2,1)S(1)}, bf16[512,128]{1,0:T(8,128)(2,1)S(1)}, u32[]{:S(2)}, u32[]{:S(2)}) collective-permute-start(bf16[512,128]{1,0:T(8,128)(2,1)S(1)} %bitcast.27), channel_id=1, source_target_pairs={{0,3},{1,0},{2,1},{3,2},{4,7},{5,4},{6,5},{7,6},{8,11},{9,8},{10,9... | collective-permute-start | bytes 393224 | tf_op jit(solution)/shard_map/ppermute | solution.py:387
  111.5 21.4 %all-to-all-start.3 = ((f32[256,1,192]{2,1,0:T(1,128)}), f32[256,1,192]{2,1,0:T(1,128)S(1)}, u32[]{:S(2)}, u32[]{:S(2)}) async-start(f32[256,1,192]{2,1,0:T(1,128)} %broadcast_in_dim.57), calls=%async_computation.3 | async-start | bytes 524288 | tf_op jit(solution)/shard_map/all_to_all | solution.py:412
  167.0 3.4 %copy-start.1 = (bf16[8,4,128,1024]{3,2,1,0:T(8,128)(2,1)S(1)}, bf16[8,4,128,1024]{3,2,1,0:T(8,128)(2,1)}, u32[]{:S(2)}) copy-start(bf16[8,4,128,1024]{3,2,1,0:T(8,128)(2,1)} %get-tuple-element.16.applied) | copy-start | bytes 25165828
